TPU v7x, 256 devices: a whole 4x4x8 slice. The times are simulated.
256 devices in a mesh: seq: 16 (over z_hi, y), head: 4 (over x), prompt: 4 (over z_lo, core).
Axes of the slice: x: 4, y: 4, z: 8 (z_hi: 4, z_lo: 2; z = z_hi * 2 + z_lo), core: 2. Of those that a mesh axis runs over, the one named last changes fastest.
Arguments:
- heads_pre: bfloat16 [8192, 16384], P(('prompt', 'seq'), 'head'), parts along dimension 0, may hold values from -6 to 6
- maps_pre: bfloat16 [8192, 2, 2048], P(('prompt', 'seq'), None, 'head'), parts along dimension 0, may hold values from -6 to 6
- step_prompt: float32 [8192, 256], P(('prompt', 'seq'), 'head'), parts along dimension 0, may hold values from 0 to 0.3, as said below
- head_rate: float32 [256], P('head'), may hold values from 0.5 to 1
- skip_gain: float32 [256], P('head'), may hold values from 0.5 to 1.5
- conv_head_taps: float32 [4, 16384], P(None, 'head'), may hold values from -3 to 3
- conv_head_bias: float32 [16384], P('head'), may hold values from -3 to 3
- conv_map_taps: float32 [4, 2, 2048], P(None, None, 'head'), may hold values from -3 to 3
- filter_mapping_offset: float32 [2, 2048], P(None, 'head'), may hold values from -3 to 3
- heads_dec: bfloat16 [64, 4, 16384], P(('prompt', 'seq'), None, 'head'), parts along dimension 0, may hold values from -6 to 6
- maps_dec: bfloat16 [64, 4, 2, 2048], P(('prompt', 'seq'), None, None, 'head'), parts along dimension 0, may hold values from -6 to 6
- step_dec: float32 [64, 4, 256], P(('prompt', 'seq'), None, 'head'), parts along dimension 0, may hold values from 0.01 to 0.3
Outputs:
- prompt_out: bfloat16 [8192, 16384], P(('prompt', 'seq'), 'head'), parts along dimension 0
- sample_out: bfloat16 [64, 4, 16384], P(('prompt', 'seq'), None, 'head'), parts along dimension 0
There are 4 independent parts, one for each index of `prompt`. A program takes and returns all parts, laid end to end along the dimension named above; an argument that names none is the same for every part. Nothing has to cross between parts.
Inputs may be any that keep to these rules, and one draw needn't show every extreme that they name: `step_prompt`: step sizes, all positive.
All inputs are finite; a program needn't handle non-finite values.
Results may differ from a plain program's by a relative error of at most 0.0035.
Values may be sent and summed in bfloat16 or wider, within the bound.
A program may use at most 192 MiB of HBM per device.

v0:
```python
import jax
import jax.numpy as jnp
from jax import lax
from jax.sharding import PartitionSpec as P

HEADS = 256
HEAD_DIM = 64
STATE = 256
GROUPS = 8
CONV = 4
BLOCK_TOKENS = 128
STEPS = 4


def from_behind(block, axis, distance):
    devices = range(lax.axis_size(axis))
    route = [(i - distance, i) for i in devices if i - distance in devices]
    return lax.ppermute(block, axis, route)


def carried_in(value, axis, join, neutral):
    count, mine = (lax.axis_size(axis), lax.axis_index(axis))
    pieces = jax.tree.map(lambda part: lax.all_gather(part, axis), value)
    subtotal = jax.tree.map(
        lambda part, zero: jnp.full_like(part, 0) + jnp.asarray(zero, part.dtype), value, neutral
    )

    def turn(position, subtotal):
        longer = join(subtotal, jax.tree.map(lambda part: part[position], pieces))
        return jax.tree.map(lambda new, old: jnp.where(position < mine, new, old), longer, subtotal)

    return lax.fori_loop(0, count - 1, turn, subtotal)


def spread(block, axis, source):
    block = jnp.where(lax.axis_index(axis) == source, block, jnp.zeros_like(block))
    return lax.psum(block, axis)


def conv_silu(padded, conv_weight, conv_bias, sequence_length):
    summed = conv_bias + conv_weight[0] * padded[0:sequence_length].astype(jnp.float32)
    for offset in range(1, CONV):
        summed = summed + conv_weight[offset] * padded[offset : offset + sequence_length].astype(
            jnp.float32
        )
    return jax.nn.silu(summed).astype(jnp.bfloat16)


def combine_pairs(former, latter):
    return (former[0] * latter[0], latter[0][..., None, None] * former[1] + latter[1])


def local(
    heads_pre,
    maps_pre,
    step_prompt,
    head_rate,
    skip_gain,
    conv_head_taps,
    conv_head_bias,
    conv_map_taps,
    filter_mapping_offset,
    heads_dec,
    maps_dec,
    step_dec,
):
    border = from_behind((heads_pre[-(CONV - 1) :], maps_pre[-(CONV - 1) :]), "seq", 1)
    sequence_length = heads_pre.shape[0]
    heads_local = step_prompt.shape[1]
    per_group = HEADS // GROUPS
    groups_local = heads_local // per_group
    x_conv = conv_silu(
        jnp.concatenate([border[0], heads_pre], 0), conv_head_taps, conv_head_bias, sequence_length
    )
    bc_conv = conv_silu(
        jnp.concatenate([border[1], maps_pre], 0),
        conv_map_taps,
        filter_mapping_offset,
        sequence_length,
    )
    blocks = sequence_length // BLOCK_TOKENS
    x_blocks = x_conv.reshape(blocks, BLOCK_TOKENS, groups_local, per_group, HEAD_DIM)
    in_maps = bc_conv[:, 0].reshape(blocks, BLOCK_TOKENS, groups_local, STATE)
    result_mappings = bc_conv[:, 1].reshape(blocks, BLOCK_TOKENS, groups_local, STATE)
    step_block_list = step_prompt.reshape(blocks, BLOCK_TOKENS, groups_local, per_group)
    decay_rate = head_rate.reshape(groups_local, per_group)
    skip_heads = skip_gain.reshape(groups_local, per_group)
    log_decay = jnp.cumsum(-step_block_list * decay_rate, axis=1)
    log_ends = log_decay[:, -1]
    log_columns = jnp.moveaxis(log_decay, 1, -1)
    logarithmic_spacings = log_columns[..., :, None] - log_columns[..., None, :]
    causal = jnp.arange(BLOCK_TOKENS)[:, None] >= jnp.arange(BLOCK_TOKENS)[None, :]
    decay_mat = jnp.exp(jnp.where(causal, logarithmic_spacings, -jnp.inf))
    scores = jnp.einsum(
        "kqgn,ksgn->kgqs", result_mappings, in_maps, preferred_element_type=jnp.float32
    )
    mixing = (
        scores[:, :, None] * decay_mat * jnp.moveaxis(step_block_list, 1, -1)[..., None, :]
    ).astype(jnp.bfloat16)
    y_inner = jnp.einsum("kgjqs,ksgjp->kqgjp", mixing, x_blocks, preferred_element_type=jnp.float32)
    weights = jnp.exp(log_ends[:, None] - log_decay) * step_block_list
    weighted = (x_blocks.astype(jnp.float32) * weights[..., None]).astype(jnp.bfloat16)
    span_states = jnp.einsum(
        "kqgjp,kqgn->kgjpn", weighted, in_maps, preferred_element_type=jnp.float32
    )
    gains = jnp.exp(log_ends)
    running = jnp.zeros((groups_local, per_group, HEAD_DIM, STATE), jnp.float32)
    leading = jnp.ones((groups_local, per_group), jnp.float32)
    entering = [running]
    leads = [leading]
    running = gains[0][..., None, None] * running + span_states[0]
    leading = leading * gains[0]
    incoming = carried_in(
        (leading, running), "seq", combine_pairs, (jnp.ones_like(leading), jnp.zeros_like(running))
    )
    entry_all = jnp.stack(entering) + jnp.stack(leads)[..., None, None] * incoming[1][None]
    entry_low = entry_all.astype(jnp.bfloat16)
    y_cross = jnp.exp(log_decay)[..., None] * jnp.einsum(
        "kqgn,kgjpn->kqgjp", result_mappings, entry_low, preferred_element_type=jnp.float32
    )
    prompt_out = (y_inner + y_cross + skip_heads[..., None] * x_blocks.astype(jnp.float32)).astype(
        jnp.bfloat16
    )
    prompt_out = prompt_out.reshape(sequence_length, heads_local * HEAD_DIM)
    tail_x = heads_pre[-(CONV - 1) :].astype(jnp.float32)
    tail_bc = maps_pre[-(CONV - 1) :].astype(jnp.float32)
    whole_state = leading[..., None, None] * incoming[1] + running
    final_state, tail_x, tail_bc = (
        spread(whole_state, "seq", lax.axis_size("seq") - 1),
        spread(tail_x, "seq", lax.axis_size("seq") - 1),
        spread(tail_bc, "seq", lax.axis_size("seq") - 1),
    )
    dx_conv = conv_silu(
        jnp.concatenate([tail_x.astype(jnp.bfloat16), heads_dec[0]], 0),
        conv_head_taps,
        conv_head_bias,
        STEPS,
    )
    dbc_conv = conv_silu(
        jnp.concatenate([tail_bc.astype(jnp.bfloat16), maps_dec[0]], 0),
        conv_map_taps,
        filter_mapping_offset,
        STEPS,
    )
    ssm_state = final_state
    rows_out = []
    for position in range(STEPS):
        x_step = dx_conv[position].reshape(groups_local, per_group, HEAD_DIM).astype(jnp.float32)
        in_step = dbc_conv[position, 0].reshape(groups_local, STATE).astype(jnp.float32)
        out_step = dbc_conv[position, 1].reshape(groups_local, STATE).astype(jnp.float32)
        step_size = step_dec[0, position].reshape(groups_local, per_group)
        ssm_state = (
            jnp.exp(-step_size * decay_rate)[..., None, None] * ssm_state
            + (step_size[..., None] * x_step)[..., None] * in_step[:, None, None, :]
        )
        output = (
            jnp.sum(ssm_state * out_step[:, None, None, :], axis=-1)
            + skip_heads[..., None] * x_step
        )
        rows_out.append(output.astype(jnp.bfloat16).reshape(heads_local * HEAD_DIM))
    sample_out = jnp.stack(rows_out)[None]
    return (prompt_out, sample_out)


def solution(mesh):
    placed = (
        P(("prompt", "seq"), "head"),
        P(("prompt", "seq"), None, "head"),
        P(("prompt", "seq"), "head"),
        P("head"),
        P("head"),
        P(None, "head"),
        P("head"),
        P(None, None, "head"),
        P(None, "head"),
        P(("prompt", "seq"), None, "head"),
        P(("prompt", "seq"), None, None, "head"),
        P(("prompt", "seq"), None, "head"),
    )
    return jax.shard_map(
        local,
        mesh=mesh,
        in_specs=placed,
        out_specs=(P(("prompt", "seq"), "head"), P(("prompt", "seq"), None, "head")),
        check_vma=False,
    )
```

profile of v0, /device:TPU:34, one launch (start us, length us, event | category | flops | bytes accessed | tf_op | source)
XLA Modules:
  0.0 1088.7 jit_solution(2239054471963597087)
XLA Ops:
  12.3 3.5 collective-permute-start
  28.2 6.1 multiply_convert_fusion.3
  37.9 43.3 %all-gather = f32[16,1,2,32]{3,2,1,0:T(2,128)S(1)} all-gather(f32[1,1,2,32]{3,2,1,0:T(2,128)S(1)} %copy-done.23), channel_id=2, replica_groups=mesh['seq'=16,'head'=4,'prompt'=4] {'seq'}, dimensions={0}, use_global_device_ids=true | all-gather | bytes 4352 | tf_op jit(solution)/shard_map/all_gather | solution.py:23
  81.2 671.9 %all-gather.4.cloned.1.call-done = f32[32,32,64,256]{3,2,1,0:T(8,128)} async-done(((f32[2,32,64,256]{3,2,1,0:T(8,128)}), f32[32,32,64,256]{3,2,1,0:T(8,128)}) %all-gather.4.cloned.1.call-update) | async-done | bytes 67108880 | tf_op jit(solution)/shard_map/all_gather | solution.py:23
  753.1 88.6 %while.14 = (s32[]{:T(128)}, f32[2,32,64,256]{3,2,1,0:T(8,128)}, s32[]{:T(128)}, f32[16,2,32]{2,1,0:T(2,128)S(1)}, f32[16,2,32,64,256]{4,3,2,1,0:T(8,128)}, /*index=5*/s32[]{:T(128)}, s32[]{:T(128)}) while((s32[]{:T(128)}, f32[2,32,64,256]{3,2,1,0:T(8,128)}, s32[]{:T(128)}, f32[16,2,32]{2,1,0:T(2,128)S(1)}, ...), condition=%wide.region_2.3_spmd.clone, body=%wide.region_1.2_spmd.clone.sunk | while | flops 4194308 | bytes 12583785 | solution.py:32
  753.1 4.7 fusion.53
  757.8 6.0 fusion.53
  763.8 6.0 fusion.53
  769.8 6.0 fusion.53
  775.8 6.0 fusion.53
  781.8 6.0 fusion.53
  787.8 6.0 fusion.53
  793.7 6.0 fusion.53
  799.7 6.0 fusion.53
  805.7 6.0 fusion.53
  811.7 6.0 fusion.53
  817.7 6.0 fusion.53
  823.7 6.0 fusion.53
  829.7 6.0 fusion.53
  835.7 6.0 fusion.53
  841.7 5.9 add_select_fusion
  848.6 110.9 %all-reduce = (bf16[3,2,512]{2,0,1:T(4,128)(2,1)S(1)}, bf16[3,4096]{1,0:T(4,128)(2,1)S(1)}) all-reduce(f32[3,2,512]{2,0,1:T(4,128)S(1)} %convert_select_fusion.1, f32[3,4096]{1,0:T(4,128)S(1)} %convert_select_fusion), channel_id=1, replica_groups=mesh['seq'=16,'head'=4,'prompt'=4] {'seq'}, use_global_device_ids=true, to_apply=%region_5.6 | all-reduce | flops 15360 | bytes 92160 | tf_op jit(solution)/shard_map/psum | solution.py:37
  965.9 106.8 %all-reduce.3.cloned.1.call-done = f32[2,32,64,256]{3,2,1,0:T(8,128)} async-done(((f32[2,32,64,256]{3,2,1,0:T(8,128)}), f32[2,32,64,256]{3,2,1,0:T(8,128)}) %all-reduce.3.cloned.1.call-update) | async-done | bytes 4194320 | tf_op jit(solution)/shard_map/psum | solution.py:37
  1072.7 7.9 multiply_reduce_fusion.1
  (137 shorter events, 29.2 us)
Async XLA Ops:
  7.2 745.9 %all-gather.4.cloned.1.call-start = ((), (), s32[]{:S(2)}) async-start(), calls=%async_computation.1 | async-start | bytes 71303168 | tf_op jit(solution)/shard_map/all_gather | solution.py:23
  7.9 8.6 copy-start.7
  7.9 17.5 %collective-permute-start.1 = (bf16[3,2,512]{2,0,1:T(4,128)(2,1)S(1)}, bf16[3,2,512]{2,0,1:T(4,128)(2,1)S(1)}, u32[]{:S(2)}, u32[]{:S(2)}) collective-permute-start(bf16[3,2,512]{2,0,1:T(4,128)(2,1)S(1)} %copy.94), channel_id=1, source_target_pairs={{0,16},{16,32},{32,48},{48,64},{64,80},{80,96},{96,112},{112,128},... | collective-permute-start | bytes 18440 | tf_op jit(solution)/shard_map/ppermute | solution.py:18
  12.3 15.4 %collective-permute-start = (bf16[3,4096]{1,0:T(4,128)(2,1)S(1)}, bf16[3,4096]{1,0:T(4,128)(2,1)S(1)}, u32[]{:S(2)}, u32[]{:S(2)}) collective-permute-start(bf16[3,4096]{1,0:T(4,128)(2,1)S(1)} %slice.134), channel_id=1, source_target_pairs={{0,16},{16,32},{32,48},{48,64},{64,80},{80,96},{96,112},{112,128},... | collective-permute-start | bytes 73736 | tf_op jit(solution)/shard_map/ppermute | solution.py:18
  16.5 11.7 %copy-start.20 = (f32[2,32]{1,0:T(2,128)}, f32[2,32]{1,0:T(2,128)S(1)}, u32[]{:S(2)}) copy-start(f32[2,32]{1,0:T(2,128)S(1)} %mul.540) | copy-start | bytes 772
  19.0 6.7 copy-start.15
  34.3 46.9 %copy-start.8 = (bf16[3,2,512]{2,1,0:T(2,128)(2,1)S(1)}, bf16[3,2,512]{2,1,0:T(2,128)(2,1)}, u32[]{:S(2)}) copy-start(bf16[3,2,512]{2,1,0:T(2,128)(2,1)} %copy-done.7) | copy-start | bytes 18436
  37.8 1034.9 %all-reduce.3.cloned.1.call-start = ((), (), s32[]{:S(2)}) async-start(), calls=%async_computation | async-start | bytes 8388608 | tf_op jit(solution)/shard_map/psum | solution.py:37
  753.1 88.6 %copy-start.22 = (f32[2,32]{1,0:T(2,128)S(1)}, f32[2,32]{1,0:T(2,128)}, u32[]{:S(2)}) copy-start(f32[2,32]{1,0:T(2,128)} %get-tuple-element.157) | copy-start | bytes 772
  847.6 111.9 %copy-start.1 = (f32[1,4096]{1,0:T(1,128)S(1)}, f32[1,4096]{1,0:T(1,128)}, u32[]{:S(2)}) copy-start(f32[1,4096]{1,0:T(1,128)} %get-tuple-element.162) | copy-start | bytes 49156
  847.6 111.9 %copy-start.2 = (f32[1,4096]{1,0:T(1,128)S(1)}, f32[1,4096]{1,0:T(1,128)}, u32[]{:S(2)}) copy-start(f32[1,4096]{1,0:T(1,128)} %get-tuple-element.163) | copy-start | bytes 49156
  847.6 111.9 %copy-start.3 = (f32[1,4096]{1,0:T(1,128)S(1)}, f32[1,4096]{1,0:T(1,128)}, u32[]{:S(2)}) copy-start(f32[1,4096]{1,0:T(1,128)} %get-tuple-element.164) | copy-start | bytes 49156
  847.6 111.9 %copy-start.6 = (f32[4096]{0:T(1024)S(1)}, f32[4096]{0:T(1024)}, u32[]{:S(2)}) copy-start(f32[4096]{0:T(1024)} %param.20) | copy-start | bytes 49156
  847.6 111.9 %copy-start.17 = (bf16[1,4,4096]{2,1,0:T(4,128)(2,1)S(1)}, bf16[1,4,4096]{2,1,0:T(4,128)(2,1)}, u32[]{:S(2)}) copy-start(bf16[1,4,4096]{2,1,0:T(4,128)(2,1)} %param.23) | copy-start | bytes 98308
  847.6 112.4 %copy-start.24 = (f32[1,4,64]{2,1,0:T(4,128)S(1)}, f32[1,4,64]{2,1,0:T(4,128)}, u32[]{:S(2)}) copy-start(f32[1,4,64]{2,1,0:T(4,128)} %param.25) | copy-start | bytes 3076
  847.6 112.9 %copy-start.10 = (f32[2,512]{1,0:T(2,128)S(1)}, f32[2,512]{1,0:T(2,128)}, u32[]{:S(2)}) copy-start(f32[2,512]{1,0:T(2,128)} %copy-done.9) | copy-start | bytes 12292
  847.6 112.9 %copy-start.12 = (f32[2,512]{1,0:T(2,128)S(1)}, f32[2,512]{1,0:T(2,128)}, u32[]{:S(2)}) copy-start(f32[2,512]{1,0:T(2,128)} %copy-done.11) | copy-start | bytes 12292
  847.6 112.9 %copy-start.14 = (f32[2,512]{1,0:T(2,128)S(1)}, f32[2,512]{1,0:T(2,128)}, u32[]{:S(2)}) copy-start(f32[2,512]{1,0:T(2,128)} %copy-done.13) | copy-start | bytes 12292
  847.7 112.9 %copy-start.16 = (f32[2,512]{1,0:T(2,128)S(1)}, f32[2,512]{1,0:T(2,128)}, u32[]{:S(2)}) copy-start(f32[2,512]{1,0:T(2,128)} %copy-done.15) | copy-start | bytes 12292
  847.7 112.9 %copy-start.18 = (f32[2,512]{1,0:T(2,128)S(1)}, f32[2,512]{1,0:T(2,128)}, u32[]{:S(2)}) copy-start(f32[2,512]{1,0:T(2,128)} %param.22) | copy-start | bytes 12292
  847.7 112.9 %copy-start.19 = (bf16[1,4,2,512]{3,2,1,0:T(2,128)(2,1)S(1)}, bf16[1,4,2,512]{3,2,1,0:T(2,128)(2,1)}, u32[]{:S(2)}) copy-start(bf16[1,4,2,512]{3,2,1,0:T(2,128)(2,1)} %param.24) | copy-start | bytes 24580
  847.7 113.1 %copy-start.25 = (f32[64]{0:T(128)S(1)}, f32[64]{0:T(128)}, u32[]{:S(2)}) copy-start(f32[64]{0:T(128)} %param.18) | copy-start | bytes 772
  847.7 113.5 %copy-start.21 = (f32[2,32]{1,0:T(2,128)S(1)}, f32[2,32]{1,0:T(2,128)}, u32[]{:S(2)}) copy-start(f32[2,32]{1,0:T(2,128)} %copy-done.20) | copy-start | bytes 772
  847.7 113.9 %copy-start.5 = (f32[128,64]{0,1:T(8,128)S(1)}, f32[128,64]{0,1:T(8,128)}, u32[]{:S(2)}) copy-start(f32[128,64]{0,1:T(8,128)} %param.16) | copy-start | bytes 98308
  (6 other events, 26.8 us)
Sparse Core Ops, SparseCore 0:
  37.9 715.1 all-gather.3
  847.9 224.8 all-reduce.2
where the time goes:
time: 1090 us
  waiting for transfers between devices  779 us (71%)
  blocking collectives  154 us (14%)
  other arithmetic  115 us (11%)
  between operations  14.5 us (1%)
  local copies, waits for them, and re-layouts  12.7 us (1%)
    all_gather x1, waiting for transfers between devices, carried_in(): pieces = jax.tree.map(lambda part: lax.all_gather(part, axis), value)  672 us
    psum x1, blocking collectives, spread(): return lax.psum(block, axis)  111 us
    psum x1, waiting for transfers between devices, spread(): return lax.psum(block, axis)  107 us
    select_n x15, other arithmetic, turn(): jnp.where(position < mine, new, old)  88.5 us
    all_gather x1, blocking collectives, carried_in(): pieces = jax.tree.map(lambda part: lax.all_gather(part, axis), value)  43.3 us
  transfers between devices with their start and end apart: 4, of which 2 were waited for; matrix products, arithmetic and copies ran while one was open for 2% of the time, Pallas kernels for 0%

commit v1 on v0

v1 whole, which is shorter than its diff:
```python
import jax
import jax.numpy as jnp
from jax import lax
from jax.sharding import PartitionSpec as P

HEADS = 256
HEAD_DIM = 64
STATE = 256
GROUPS = 8
CONV = 4
BLOCK = 128
STEPS = 4
NEAR = 4
FAR = 4
NEAR_GROUPS = [[FAR_ * NEAR + i for i in range(NEAR)] for FAR_ in range(FAR)]
FAR_GROUPS = [[FAR_ * NEAR + i for FAR_ in range(FAR)] for i in range(NEAR)]
HL = 16
XC = HL * HEAD_DIM
f32 = jnp.float32
bf16 = jnp.bfloat16


def conv_silu(padded, taps, bias, length):
    summed = bias + taps[0] * padded[0:length].astype(f32)
    for offset in range(1, CONV):
        summed = summed + taps[offset] * padded[offset : offset + length].astype(f32)
    return jax.nn.silu(summed).astype(bf16)


def local(hp, mp, sp, rate, skip, ht, hb, mt, mb, hd, md, sd):
    me = lax.axis_index("seq")
    near = me % NEAR
    far = me // NEAR
    group = near // 2
    xin = jnp.concatenate([hp, hd[0]], 0).reshape(BLOCK + STEPS, NEAR, XC)
    maps = jnp.concatenate([mp, md[0]], 0).reshape(BLOCK + STEPS, 2, 2, STATE)
    maps = jnp.repeat(jnp.swapaxes(maps, 1, 2), 2, axis=1).reshape(BLOCK + STEPS, NEAR, 2 * STATE)
    packed = jnp.swapaxes(jnp.concatenate([xin, maps], -1), 0, 1)
    steps = jnp.concatenate([sp, sd[0]], 0).reshape(BLOCK + STEPS, NEAR, HL)
    steps = jnp.swapaxes(steps, 0, 1)
    packed = lax.all_to_all(packed, "seq", 0, 0, axis_index_groups=NEAR_GROUPS)
    steps = lax.all_to_all(steps, "seq", 0, 0, axis_index_groups=NEAR_GROUPS)

    pick = lambda a, axis, n: lax.dynamic_slice_in_dim(a, near * n, n, axis)
    rate = pick(rate, 0, HL)
    skip = pick(skip, 0, HL)
    mslice = lambda a: lax.dynamic_slice_in_dim(a, group * STATE, STATE, a.ndim - 1)
    taps = jnp.concatenate([pick(ht, 1, XC), mslice(mt).reshape(CONV, 2 * STATE)], 1)
    bias = jnp.concatenate([pick(hb, 0, XC), mslice(mb).reshape(2 * STATE)], 0)

    rows = packed[:, :BLOCK].reshape(NEAR * BLOCK, -1)
    ends = lax.all_gather(rows[-(CONV - 1) :], "seq", axis_index_groups=FAR_GROUPS)
    before = lax.dynamic_index_in_dim(ends, jnp.maximum(far - 1, 0), 0, keepdims=False)
    before = jnp.where(far > 0, before, jnp.zeros_like(before))
    tail = ends[FAR - 1]
    conv = conv_silu(jnp.concatenate([before, rows], 0), taps, bias, NEAR * BLOCK)
    xb = conv[:, :XC].reshape(NEAR, BLOCK, HL, HEAD_DIM)
    bm = conv[:, XC : XC + STATE].reshape(NEAR, BLOCK, STATE)
    cm = conv[:, XC + STATE :].reshape(NEAR, BLOCK, STATE)
    st = steps[:, :BLOCK]
    logd = jnp.cumsum(-st * rate, axis=1)
    last = logd[:, -1]
    weights = jnp.exp(last[:, None] - logd) * st
    weighted = (xb.astype(f32) * weights[..., None]).astype(bf16)
    bstate = jnp.einsum("cshp,csn->chpn", weighted, bm, preferred_element_type=f32)
    gains = jnp.exp(last)
    inner = [jnp.zeros_like(bstate[0])]
    lead = [jnp.ones_like(gains[0])]
    for c in range(NEAR):
        inner.append(gains[c][:, None, None] * inner[-1] + bstate[c])
        lead.append(lead[-1] * gains[c])
    all_states = lax.all_gather(inner[-1], "seq", axis_index_groups=FAR_GROUPS)
    all_leads = lax.all_gather(lead[-1], "seq", axis_index_groups=FAR_GROUPS)

    cols = jnp.moveaxis(logd, 1, -1)
    gap = cols[..., :, None] - cols[..., None, :]
    causal = jnp.arange(BLOCK)[:, None] >= jnp.arange(BLOCK)[None, :]
    decay = jnp.exp(jnp.where(causal, gap, -jnp.inf))
    scores = jnp.einsum("cqn,csn->cqs", cm, bm, preferred_element_type=f32)
    mixing = (scores[:, None] * decay * jnp.moveaxis(st, 1, -1)[..., None, :]).astype(bf16)
    y = jnp.einsum("chqs,cshp->cqhp", mixing, xb, preferred_element_type=f32)
    y = y + skip[:, None] * xb.astype(f32)

    drows = packed[:, BLOCK:]
    dpad = jnp.concatenate([jnp.broadcast_to(tail[None], (NEAR,) + tail.shape), drows], 1)
    dconv = jax.vmap(lambda p: conv_silu(p, taps, bias, STEPS))(dpad)
    dx = dconv[..., :XC].reshape(NEAR, STEPS, HL, HEAD_DIM).astype(f32)
    db = dconv[..., XC : XC + STATE]
    dc = dconv[..., XC + STATE :]
    ds = steps[:, BLOCK:]
    dlog = jnp.cumsum(-ds * rate, axis=1)
    dgap = dlog[:, :, None] - dlog[:, None, :]
    dcausal = jnp.arange(STEPS)[:, None] >= jnp.arange(STEPS)[None, :]
    ddecay = jnp.exp(jnp.where(dcausal[..., None], dgap, -jnp.inf)) * ds[:, None]
    dscore = jnp.sum(dc[:, :, None].astype(f32) * db[:, None].astype(f32), -1)
    dmix = dscore[..., None] * ddecay
    dy = jnp.sum(dmix[..., None] * dx[:, None], 2) + skip[:, None] * dx

    entry = jnp.zeros_like(all_states[0])
    state = jnp.zeros_like(entry)
    for g in range(FAR):
        state = all_leads[g][:, None, None] * state + all_states[g]
        entry = jnp.where(far == g + 1, state, entry)
    low = jnp.stack(
        [(lead[c][:, None, None] * entry + inner[c]).astype(bf16) for c in range(NEAR)]
    )
    cross = jnp.einsum("cqn,chpn->cqhp", cm, low, preferred_element_type=f32)
    out = (y + jnp.exp(logd)[..., None] * cross).astype(bf16).reshape(NEAR, BLOCK, XC)
    high = lax.reduce_precision(state, 8, 7)
    dcross = jnp.einsum("rkn,hpn->rkhp", dc, high.astype(bf16), preferred_element_type=f32)
    dcross = dcross + jnp.einsum(
        "rkn,hpn->rkhp", dc, (state - high).astype(bf16), preferred_element_type=f32
    )
    dout = (dy + jnp.exp(dlog)[..., None] * dcross).astype(bf16).reshape(NEAR, STEPS, XC)
    back = jnp.concatenate([out, dout], 1)
    back = lax.all_to_all(back, "seq", 0, 0, axis_index_groups=NEAR_GROUPS)
    back = jnp.swapaxes(back, 0, 1).reshape(BLOCK + STEPS, NEAR * XC)
    return back[:BLOCK], back[BLOCK:][None]


def solution(mesh):
    placed = (
        P(("prompt", "seq"), "head"),
        P(("prompt", "seq"), None, "head"),
        P(("prompt", "seq"), "head"),
        P("head"),
        P("head"),
        P(None, "head"),
        P("head"),
        P(None, None, "head"),
        P(None, "head"),
        P(("prompt", "seq"), None, "head"),
        P(("prompt", "seq"), None, None, "head"),
        P(("prompt", "seq"), None, "head"),
    )
    return jax.shard_map(
        local,
        mesh=mesh,
        in_specs=placed,
        out_specs=(P(("prompt", "seq"), "head"), P(("prompt", "seq"), None, "head")),
        check_vma=False,
    )
```

time: 1090 us -> 202 us (0.19)
  waiting for transfers between devices: 779 us -> 81 us
  blocking collectives: 154 us -> 47.3 us
  other arithmetic: 115 us -> 19 us
    all_gather x1, waiting for transfers between devices: 672 us -> 63.7 us  [local(): all_states = lax.all_gather(inner[-1], 'seq', axis_index_groups=FAR_GROUPS)]
    psum x1 -> x0, blocking collectives: 111 us -> none  [spread(): return lax.psum(block, axis)]
    psum x1 -> x0, waiting for transfers between devices: 107 us -> none  [spread(): return lax.psum(block, axis)]
    select_n x18 -> x0, other arithmetic: 95.3 us -> none  [the longest x15 88.5 us: turn(): jnp.where(position < mine, new, old)]
    all_to_all x0 -> x1, blocking collectives: none -> 20 us  [local(): back = lax.all_to_all(back, 'seq', 0, 0, axis_index_groups=NEAR_GROUPS)]
    all_to_all x0 -> x2, waiting for transfers between devices: none -> 17.2 us  [the longest x1 17.2 us: local(): packed = lax.all_to_all(packed, 'seq', 0, 0, axis_index_groups=NEAR_GROUPS)]
    all_gather x1 -> x2, blocking collectives: 43.3 us -> 27.3 us  [the longest x1 16.4 us: local(): lax.all_gather(rows[-(CONV - 1):], 'seq', axis_index_groups=FAR_GROUPS)]
  transfers between devices with their start and end apart: 4 -> 3, of which waited for: 2 -> 2; matrix products, arithmetic and copies ran while one was open for 2% -> 10% of each run, Pallas kernels for 0% -> 0%
where the time goes in v1:
time: 202 us; the launch traced here: 201 us
  waiting for transfers between devices  81 us (40%)
  blocking collectives  47.3 us (23%)
  local copies, waits for them, and re-layouts  22.1 us (11%)
  other arithmetic  19 us (9%)
  between operations  14.8 us (7%)
  starting transfers between devices  9.27 us (5%)
  matrix products  7.39 us (4%)
    all_gather x1, waiting for transfers between devices, local(): all_states = lax.all_gather(inner[-1], 'seq', axis_index_groups=FAR_GROUPS)  63.7 us
    all_to_all x1, blocking collectives, local(): back = lax.all_to_all(back, 'seq', 0, 0, axis_index_groups=NEAR_GROUPS)  20 us
    all_to_all x1, waiting for transfers between devices, local(): packed = lax.all_to_all(packed, 'seq', 0, 0, axis_index_groups=NEAR_GROUPS)  17.2 us
    all_gather x1, blocking collectives, local(): lax.all_gather(rows[-(CONV - 1):], 'seq', axis_index_groups=FAR_GROUPS)  16.4 us
    all_gather x1, blocking collectives, local(): all_leads = lax.all_gather(lead[-1], 'seq', axis_index_groups=FAR_GROUPS)  10.8 us
    unnamed x73, local copies, waits for them, and re-layouts  7.09 us
    all_to_all x1, starting transfers between devices, local(): packed = lax.all_to_all(packed, 'seq', 0, 0, axis_index_groups=NEAR_GROUPS)  4.81 us
    all_to_all x1, starting transfers between devices, local(): steps = lax.all_to_all(steps, 'seq', 0, 0, axis_index_groups=NEAR_GROUPS)  4.46 us
  transfers between devices with their start and end apart: 3, of which 2 were waited for; matrix products, arithmetic and copies ran while one was open for 10% of the time, Pallas kernels for 0%

profile of v1, /device:TPU:34, one launch (start us, length us, event | category | flops | bytes accessed | tf_op | source)
XLA Modules:
  0.0 200.9 jit_solution(8362098163128413860)
XLA Ops:
  8.0 1.4 maximum_bitcast_fusion.2
  9.4 4.5 %all-to-all-start.1 = ((f32[4,132,16]{1,2,0:T(8,128)}), f32[4,132,16]{1,2,0:T(8,128)S(1)}, u32[]{:S(2)}, u32[]{:S(2)}) async-start(f32[4,132,16]{1,2,0:T(8,128)} %maximum_bitcast_fusion.2), calls=%async_computation.1 | async-start | bytes 131072 | tf_op jit(solution)/shard_map/all_to_all | solution.py:42
  14.5 1.1 concatenate.47
  16.9 1.6 copy.89
  19.2 1.3 maximum_bitcast_fusion
  20.6 4.8 %all-to-all-start = ((bf16[4,132,1536]{2,1,0:T(8,128)(2,1)}), bf16[4,132,1536]{2,1,0:T(8,128)(2,1)S(1)}, u32[]{:S(2)}, u32[]{:S(2)}) async-start(bf16[4,132,1536]{2,1,0:T(8,128)(2,1)} %maximum_bitcast_fusion), calls=%async_computation | async-start | bytes 3342336 | tf_op jit(solution)/shard_map/all_to_all | solution.py:41
  29.4 17.2 %all-to-all-done = bf16[4,132,1536]{2,1,0:T(8,128)(2,1)S(1)} async-done(((bf16[4,132,1536]{2,1,0:T(8,128)(2,1)}), bf16[4,132,1536]{2,1,0:T(8,128)(2,1)S(1)}, u32[]{:S(2)}, u32[]{:S(2)}) %all-to-all-start) | async-done | bytes 1622048 | tf_op jit(solution)/shard_map/all_to_all | solution.py:41
  46.7 16.4 %all-gather.1 = bf16[4,3,1536]{2,1,0:T(4,128)(2,1)S(1)} all-gather(bf16[1,3,1536]{2,1,0:T(4,128)(2,1)S(1)} %slice_bitcast_fusion.1), channel_id=2, replica_groups={{0,64,128,192},{16,80,144,208},{32,96,160,224},{48,112,176,240},{1,65,1..., dimensions={0}, use_global_device_ids=true | all-gather | bytes 46080 | tf_op jit(solution)/shard_map/all_gather | solution.py:52
  63.8 2.2 %multiply_convert_fusion.1 = bf16[512,1536]{1,0:T(8,128)(2,1)S(1)} fusion(bf16[512,1536]{1,0:T(8,128)(2,1)S(1)} %bitcast.117, bf16[3,1536]{1,0:T(4,128)(2,1)S(1)} %get-tuple-element.30, f32[1536]{0:T(1024)S(1)} %get-tuple-element.8, f32[1536]{0:T(1024)S(1)} %get-tuple-element.9, f32[1536]{0:T(1024)S(1)} %get-tuple-element.7, f32[1536]{0:T(1024)S(1)} %get-tuple-element.6, ...), kind=kLoop, calls=%fused_computation.1 | loop fusion | flops 20447232 | bytes 3185664 | tf_op jit(solution)/shard_map/convert_element_type | solution.py:27
  67.1 1.3 reshape.151
  68.4 1.8 copy.98
  70.2 1.7 fusion.27
  72.0 1.4 slice_add_fusion
  77.2 10.8 %all-gather.2 = f32[4,1,16]{2,1,0:T(1,128)S(1)} all-gather(f32[1,1,16]{2,1,0:T(1,128)} %get-tuple-element.33), channel_id=1, replica_groups={{0,64,128,192},{16,80,144,208},{32,96,160,224},{48,112,176,240},{1,65,1..., dimensions={0}, use_global_device_ids=true | all-gather | bytes 320 | tf_op jit(solution)/shard_map/all_gather | solution.py:73
  88.0 0.9 slice.213
  90.7 4.1 %fusion = f32[4,16,64,128]{3,2,1,0:T(8,128)} fusion(bf16[4,128,16,64]{1,3,2,0:T(8,128)(2,1)S(1)} %copy.98, f32[4,16,128]{2,1,0:T(8,128)S(1)} %copy-done.16, f32[4,16,128]{2,1,0:T(8,128)S(1)} %copy.95, f32[4,128,128]{2,1,0:T(8,128)S(1)} %fusion.62, pred[128,128]{1,0:T(8,128)(4,1)} %iota_compare_fusion), kind=kOutput, calls=%fused_computation.6 | convolution fusion | flops 139460608 | bytes 3489792 | tf_op jit(solution)/shard_map/chqs,cshp->cqhp/dot_general | solution.py:81
  94.8 63.7 %all-gather.5.cloned.1.call-done = f32[4,16,64,256]{3,2,1,0:T(8,128)} async-done(((f32[1,16,64,256]{3,2,1,0:T(8,128)}), f32[4,16,64,256]{3,2,1,0:T(8,128)}) %all-gather.5.cloned.1.call-update) | async-done | bytes 4194320 | tf_op jit(solution)/shard_map/all_gather | solution.py:72
  158.6 2.5 %bitcast_add_fusion = f32[16,64,256]{2,1,0:T(8,128)S(1)} fusion(f32[4,16,64,256]{3,2,1,0:T(8,128)} %all-gather.5.cloned.1.call-done, f32[16]{0:T(128)S(1)} %get-tuple-element.40, f32[16]{0:T(128)S(1)} %get-tuple-element.38, f32[16]{0:T(128)S(1)} %get-tuple-element.39, f32[16]{0:T(128)S(1)} %get-tuple-element.37), kind=kLoop, calls=%fused_computation.42 | loop fusion | flops 1835008 | bytes 5243136 | tf_op jit(solution)/shard_map/add | solution.py:102
  162.0 3.0 %fusion.58 = (bf16[1,16,64,256]{3,2,1,0:T(8,128)(2,1)S(1)}, f32[1,16,64,256]{3,2,1,0:T(8,128)S(1)}) fusion(pred[]{:T(512)S(6)} %eq.17, pred[]{:T(512)S(6)} %eq.16, pred[]{:T(512)S(6)} %eq.15, f32[4,16,64,256]{3,2,1,0:T(8,128)} %all-gather.5.cloned.1.call-done, f32[16]{0:T(128)S(1)} %get-tuple-element.40, f32[16]{0:T(128)S(1)} %get-tuple-element.38, ...), kind=kLoop, calls=%fused_computation.123 | loop fusion | flops 3145728 | bytes 5767428 | tf_op jit(solution)/shard_map/convert_element_type | solution.py:105
  168.2 20.0 %all_to_all.15 = bf16[4,132,1024]{2,1,0:T(8,128)(2,1)S(1)} all-to-all(bf16[4,132,1024]{2,1,0:T(8,128)(2,1)S(1)} %pad_maximum_fusion.1), channel_id=1, replica_groups={{0,16,32,48},{64,80,96,112},{128,144,160,176},{192,208,224,240},{1,17,3..., dimensions={0} | all-to-all | bytes 2162688 | tf_op jit(solution)/shard_map/all_to_all | solution.py:116
  188.2 1.3 copy.109
  189.5 1.2 slice.222
  190.8 2.3 %copy.110 = bf16[128,4096]{1,0:T(8,128)(2,1)} copy(bf16[128,4096]{0,1:T(8,128)(2,1)} %bitcast.119) | data formatting | bytes 2097152
  193.1 1.0 copy.111
  (128 shorter events, 18.4 us)
Async XLA Ops:
  7.2 12.0 %copy-start = (f32[4,4096]{1,0:T(4,128)S(1)}, f32[4,4096]{1,0:T(4,128)}, u32[]{:S(2)}) copy-start(f32[4,4096]{1,0:T(4,128)} %param.17) | copy-start | bytes 196612
  9.4 11.2 %all-to-all-start.1 = ((f32[4,132,16]{1,2,0:T(8,128)}), f32[4,132,16]{1,2,0:T(8,128)S(1)}, u32[]{:S(2)}, u32[]{:S(2)}) async-start(f32[4,132,16]{1,2,0:T(8,128)} %maximum_bitcast_fusion.2), calls=%async_computation.1 | async-start | bytes 131072 | tf_op jit(solution)/shard_map/all_to_all | solution.py:42
  16.3 2.9 %copy-start.15 = (bf16[1,4,4096]{2,1,0:T(4,128)(2,1)S(1)}, bf16[1,4,4096]{2,1,0:T(4,128)(2,1)}, u32[]{:S(2)}) copy-start(bf16[1,4,4096]{2,1,0:T(4,128)(2,1)} %param.21) | copy-start | bytes 98308
  19.2 6.2 %dynamic-slice-start = ((f32[4096]{0:T(1024)}, s32[]{:T(128)}), f32[1024]{0:T(1024)S(1)}, s32[]{:S(2)}) async-start(f32[4096]{0:T(1024)} %param.18, s32[]{:T(128)} %select_n.94), calls=%async_computation.4 | async-start | bytes 8704 | tf_op jit(solution)/shard_map/dynamic_slice | solution.py:44
  19.2 6.2 %copy-start.29 = (f32[64]{0:T(128)S(1)}, f32[64]{0:T(128)}, u32[]{:S(2)}) copy-start(f32[64]{0:T(128)} %param.15) | copy-start | bytes 772
  20.6 26.0 %all-to-all-start = ((bf16[4,132,1536]{2,1,0:T(8,128)(2,1)}), bf16[4,132,1536]{2,1,0:T(8,128)(2,1)S(1)}, u32[]{:S(2)}, u32[]{:S(2)}) async-start(bf16[4,132,1536]{2,1,0:T(8,128)(2,1)} %maximum_bitcast_fusion), calls=%async_computation | async-start | bytes 3342336 | tf_op jit(solution)/shard_map/all_to_all | solution.py:41
  25.4 133.2 %all-gather.5.cloned.1.call-start = ((), (), s32[]{:S(2)}) async-start(), calls=%async_computation.3 | async-start | bytes 5242880 | tf_op jit(solution)/shard_map/all_gather | solution.py:72
  25.6 40.5 %copy-start.8 = (f32[1536]{0:T(1024)}, f32[1536]{0:T(1024)S(1)}, u32[]{:S(2)}) copy-start(f32[1536]{0:T(1024)S(1)} %get-tuple-element.7) | copy-start | bytes 18436
  25.6 40.5 %copy-start.10 = (f32[1536]{0:T(1024)}, f32[1536]{0:T(1024)S(1)}, u32[]{:S(2)}) copy-start(f32[1536]{0:T(1024)S(1)} %get-tuple-element.8) | copy-start | bytes 18436
  25.6 40.5 %copy-start.12 = (f32[1536]{0:T(1024)}, f32[1536]{0:T(1024)S(1)}, u32[]{:S(2)}) copy-start(f32[1536]{0:T(1024)S(1)} %get-tuple-element.9) | copy-start | bytes 18436
  46.6 19.5 %copy-start.3 = (bf16[4,132,1536]{2,1,0:T(8,128)(2,1)}, bf16[4,132,1536]{2,1,0:T(8,128)(2,1)S(1)}, u32[]{:S(2)}) copy-start(bf16[4,132,1536]{2,1,0:T(8,128)(2,1)S(1)} %all-to-all-done) | copy-start | bytes 4866052
  72.0 4.1 %copy-start.21 = (f32[16]{0:T(128)S(1)}, f32[16]{0:T(128)}, u32[]{:S(2)}) copy-start(f32[16]{0:T(128)} %copy-done.20) | copy-start | bytes 196
  72.0 5.1 %copy-start.7 = (f32[4,128,16]{2,1,0:T(8,128)S(1)}, f32[4,128,16]{2,1,0:T(8,128)}, u32[]{:S(2)}) copy-start(f32[4,128,16]{2,1,0:T(8,128)} %get-tuple-element.21) | copy-start | bytes 98308
  72.0 17.0 %copy-start.14 = (bf16[3,1536]{1,0:T(4,128)(2,1)S(1)}, bf16[3,1536]{1,0:T(4,128)(2,1)}, u32[]{:S(2)}) copy-start(bf16[3,1536]{1,0:T(4,128)(2,1)} %get-tuple-element.29) | copy-start | bytes 27652
  72.0 17.0 %copy-start.9 = (f32[1536]{0:T(1024)S(1)}, f32[1536]{0:T(1024)}, u32[]{:S(2)}) copy-start(f32[1536]{0:T(1024)} %copy-done.8) | copy-start | bytes 18436
  72.0 17.0 %copy-start.11 = (f32[1536]{0:T(1024)S(1)}, f32[1536]{0:T(1024)}, u32[]{:S(2)}) copy-start(f32[1536]{0:T(1024)} %copy-done.10) | copy-start | bytes 18436
  72.0 17.0 %copy-start.13 = (f32[1536]{0:T(1024)S(1)}, f32[1536]{0:T(1024)}, u32[]{:S(2)}) copy-start(f32[1536]{0:T(1024)} %copy-done.12) | copy-start | bytes 18436
  72.0 18.4 %copy-start.4 = (bf16[512,256]{1,0:T(8,128)(2,1)S(1)}, bf16[512,256]{1,0:T(8,128)(2,1)}, u32[]{:S(2)}) copy-start(bf16[512,256]{1,0:T(8,128)(2,1)} %get-tuple-element.20) | copy-start | bytes 786436
  72.0 18.4 %copy-start.5 = (bf16[512,256]{1,0:T(8,128)(2,1)S(1)}, bf16[512,256]{1,0:T(8,128)(2,1)}, u32[]{:S(2)}) copy-start(bf16[512,256]{1,0:T(8,128)(2,1)} %get-tuple-element.19) | copy-start | bytes 786436
  74.2 16.5 %copy-start.16 = (f32[4,16,128]{2,1,0:T(8,128)S(1)}, f32[4,16,128]{2,1,0:T(8,128)}, u32[]{:S(2)}) copy-start(f32[4,16,128]{2,1,0:T(8,128)} %get-tuple-element.23) | copy-start | bytes 98308
  161.8 3.2 %copy-start.22 = (f32[16]{0:T(128)S(1)}, f32[16]{0:T(128)}, u32[]{:S(2)}) copy-start(f32[16]{0:T(128)} %get-tuple-element.31) | copy-start | bytes 196
  161.8 3.2 %copy-start.25 = (f32[16]{0:T(128)S(1)}, f32[16]{0:T(128)}, u32[]{:S(2)}) copy-start(f32[16]{0:T(128)} %get-tuple-element.12) | copy-start | bytes 196
  161.8 3.2 %copy-start.26 = (f32[16]{0:T(128)S(1)}, f32[16]{0:T(128)}, u32[]{:S(2)}) copy-start(f32[16]{0:T(128)} %get-tuple-element.13) | copy-start | bytes 196
  162.0 3.5 %copy-start.2 = (f32[4,16,64,256]{3,2,1,0:T(8,128)S(1)}, f32[4,16,64,256]{3,2,1,0:T(8,128)}, u32[]{:S(2)}) copy-start(f32[4,16,64,256]{3,2,1,0:T(8,128)} %copy-done.1) | copy-start | bytes 12582916
  (12 other events, 22.9 us)
Sparse Core Ops, SparseCore 0:
  74.3 84.1 all-gather.4
